TPU v7x, 512 devices: a whole 4x8x8 slice. The times are simulated.
512 devices in a mesh: blk: 32 (over x, y_hi, core), grp: 16 (over z, y_lo).
Axes of the slice: x: 4, y: 8 (y_hi: 4, y_lo: 2; y = y_hi * 2 + y_lo), z: 8, core: 2. Of those that a mesh axis runs over, the one named last changes fastest.
Arguments:
- amplitudes: bfloat16 [4096, 8, 4, 128], P('blk'), may hold values from -6 to 6
- integrals: bfloat16 [256, 4096, 128], P('grp', 'blk'), may hold values from -0.15625 to 0.15625
- virt_energy: float32 [4096], replicated, may hold values from 0.5 to 4
- pair_energy: float32 [8], replicated, may hold values from -3 to -0.5
- offsets: int32 [32, 4], replicated, may hold values from 0 to 31, as said below
Outputs:
- ladder: float32 [4096, 8, 4, 128], P(('blk', 'grp'))
- new_amplitudes: float32 [4096, 8, 4, 128], P(('blk', 'grp'))
Inputs may be any that keep to these rules, and one draw needn't show every extreme that they name: The 4 offsets of one row tile are different; the first 3 are at most 2, the last is larger than 2.
All inputs are finite; a program needn't handle non-finite values.
Results may differ from a plain program's by a relative error of at most 0.0029.
Values may be sent and summed in bfloat16 or wider, within the bound.
No kernel may reach another device: no remote copies, remote signals or barrier semaphores. Data moves between devices by JAX's collectives and lax.ppermute only.
A program may use at most 64 MiB of HBM per device.

v0:
```python
import jax
import jax.numpy as jnp
from jax import lax
from jax.sharding import PartitionSpec as P


def in_blocks(x, dim, devices):
    before, after = (x.shape[:dim], x.shape[dim + 1 :])
    return jnp.moveaxis(x.reshape(*before, devices, -1, *after), dim, 0)


def sum_at_owner(x, axis, dim):
    devices = lax.axis_size(axis)
    blocks = lax.all_to_all(in_blocks(x, dim, devices), axis, 0, 0, tiled=True)
    return jnp.sum(blocks, axis=0)


def local(amplitudes, integrals, virt_energy, pair_energy, offsets):
    tiles = lax.axis_size("blk")
    tile_index = lax.axis_index("blk")
    group_index = lax.axis_index("grp")
    slab_width = integrals.shape[2]
    aux_local = integrals.shape[0]
    pair_count = amplitudes.shape[1]
    slot_count = amplitudes.shape[2]
    own_offsets = lax.dynamic_slice_in_dim(offsets, tile_index, 1, 0)[0]
    cols = (tile_index - own_offsets) % tiles
    piece = lax.all_gather(integrals, "blk", axis=1, tiled=True)
    count = piece.shape[1] // slab_width
    tile_ids = jnp.arange(count, dtype=jnp.int32)
    onehot = (cols[:, None] == tile_ids[None, :]).astype(jnp.bfloat16)
    pieces = piece.reshape(aux_local, count, slab_width, slab_width)
    chosen = jnp.einsum("sj,qjbd->qsbd", onehot, pieces, preferred_element_type=jnp.float32)
    col_blocks = chosen.astype(jnp.bfloat16)
    flattened_rows = amplitudes.reshape(slab_width, pair_count * slot_count * slab_width)
    rows_per_device = slab_width // lax.axis_size("grp")

    def add_aux(aux, total):
        half_split = jnp.dot(
            integrals[aux], flattened_rows, preferred_element_type=jnp.float32
        ).astype(jnp.bfloat16)
        half_split = half_split.reshape(
            rows_per_device * lax.axis_size("grp"), pair_count, slot_count, slab_width
        )
        return total + jnp.einsum(
            "apsd,sbd->apsb", half_split, col_blocks[aux], preferred_element_type=jnp.float32
        )

    total_start_offset = jnp.zeros(
        (rows_per_device * lax.axis_size("grp"), pair_count, slot_count, slab_width), jnp.float32
    )
    ladder = sum_at_owner(lax.fori_loop(0, aux_local, add_aux, total_start_offset), "grp", 0)
    first_row = group_index * rows_per_device
    old_rows = lax.dynamic_slice_in_dim(amplitudes, first_row, rows_per_device, 0).astype(
        jnp.float32
    )
    row_energy = lax.dynamic_slice_in_dim(
        virt_energy, tile_index * slab_width + first_row, rows_per_device, 0
    )
    table = virt_energy.reshape(tiles, slab_width)
    selector = (cols[:, None] == jnp.arange(tiles, dtype=jnp.int32)[None, :]).astype(jnp.float32)
    col_energy = jnp.dot(selector, table, precision=lax.Precision.HIGHEST)
    denom = (
        row_energy[:, None, None, None]
        + col_energy[None, None, :, :]
        - pair_energy[None, :, None, None]
    )
    new_amplitudes = old_rows - ladder / denom
    return (ladder, new_amplitudes)


def solution(mesh):
    placed = (P("blk", None, None, None), P("grp", "blk", None), P(), P(), P())
    return jax.shard_map(
        local,
        mesh=mesh,
        in_specs=placed,
        out_specs=(P(("blk", "grp"), None, None, None), P(("blk", "grp"), None, None, None)),
        check_vma=False,
    )
```

profile of v0, /device:TPU:2, one launch (start us, length us, event | category | flops | bytes accessed | tf_op | source)
XLA Modules:
  0.0 332.7 jit_solution(4653998717116399375)
XLA Ops:
  7.9 1.8 reshape.51
  10.0 128.9 %all-gather.2.cloned.1.call-done = bf16[16,4096,128]{2,1,0:T(8,128)(2,1)} async-done(((bf16[16,128,128]{2,1,0:T(8,128)(2,1)}), bf16[16,4096,128]{2,1,0:T(8,128)(2,1)}) %all-gather.2.cloned.1.call-update) | async-done | bytes 16777232 | tf_op jit(solution)/shard_map/all_gather | solution.py:28
  138.9 16.6 %convert_bitcast_fusion = bf16[16,4,128,128]{3,1,2,0:T(4,128)(2,1)} fusion(bf16[16,32,128,128]{3,2,1,0:T(8,128)(2,1)} %bitcast.32, s32[4]{0:T(128)S(1)} %and_select_fusion), kind=kOutput, calls=%fused_computation.10 | convolution fusion | flops 68157568 | bytes 18874384 | tf_op jit(solution)/shard_map/sj,qjbd->qsbd/dot_general | solution.py:33
  155.5 105.9 %while.14 = (s32[]{:T(128)}, f32[128,8,4,128]{0,3,1,2:T(8,128)}, bf16[16,4,128,128]{3,1,2,0:T(4,128)(2,1)}, bf16[16,128,128]{2,1,0:T(8,128)(2,1)}, bf16[128,4096]{1,0:T(8,128)(2,1)S(1)}, /*index=5*/s32[]{:T(128)}, s32[]{:T(128)}) while((s32[]{:T(128)}, f32[128,8,4,128]{0,3,1,2:T(8,128)}, bf16[16,4,128,128]{3,1,2,0:T(4,128)(2,1)}, ...), condition=%wide.region_1.2_spmd.clone, body=%wide.region_0.1_spmd.clone.sunk | while | flops 270008320 | bytes 9863271 | solution.py:52
  155.5 0.9 constant_dynamic-slice_fusion.3
  156.4 1.2 convolution_convert_fusion.2
  158.4 2.2 bitcast_add_fusion.2
  160.6 0.9 constant_dynamic-slice_fusion.3
  161.6 1.2 convolution_convert_fusion.2
  163.5 3.8 %bitcast_add_fusion.2 = f32[128,8,4,128]{0,3,1,2:T(8,128)} fusion(f32[128,8,4,128]{0,3,1,2:T(8,128)} %get-tuple-element.181, bf16[128,8,4,128]{3,2,1,0:T(4,128)(2,1)S(1)} %reshape.59, pred[]{:T(512)S(6)} %compare.7, bf16[1,4,128,128]{3,1,2,0:T(4,128)(2,1)S(1)} %constant_dynamic-slice_fusion.3), kind=kOutput, calls=%fused_computation.1.clone.1 | convolution fusion | flops 135266304 | bytes 5373953 | tf_op jit(solution)/shard_map/while/body/eval_jaxpr/apsd,sbd->apsb/dot_general | solution.py:45
  167.3 0.9 constant_dynamic-slice_fusion.3
  168.3 1.2 convolution_convert_fusion.2
  170.2 3.8 %bitcast_add_fusion.2 = f32[128,8,4,128]{0,3,1,2:T(8,128)} fusion(f32[128,8,4,128]{0,3,1,2:T(8,128)} %get-tuple-element.181, bf16[128,8,4,128]{3,2,1,0:T(4,128)(2,1)S(1)} %reshape.59, pred[]{:T(512)S(6)} %compare.7, bf16[1,4,128,128]{3,1,2,0:T(4,128)(2,1)S(1)} %constant_dynamic-slice_fusion.3), kind=kOutput, calls=%fused_computation.1.clone.1 | convolution fusion | flops 135266304 | bytes 5373953 | tf_op jit(solution)/shard_map/while/body/eval_jaxpr/apsd,sbd->apsb/dot_general | solution.py:45
  174.0 0.9 constant_dynamic-slice_fusion.3
  175.0 1.2 convolution_convert_fusion.2
  177.0 3.8 %bitcast_add_fusion.2 = f32[128,8,4,128]{0,3,1,2:T(8,128)} fusion(f32[128,8,4,128]{0,3,1,2:T(8,128)} %get-tuple-element.181, bf16[128,8,4,128]{3,2,1,0:T(4,128)(2,1)S(1)} %reshape.59, pred[]{:T(512)S(6)} %compare.7, bf16[1,4,128,128]{3,1,2,0:T(4,128)(2,1)S(1)} %constant_dynamic-slice_fusion.3), kind=kOutput, calls=%fused_computation.1.clone.1 | convolution fusion | flops 135266304 | bytes 5373953 | tf_op jit(solution)/shard_map/while/body/eval_jaxpr/apsd,sbd->apsb/dot_general | solution.py:45
  180.8 0.9 constant_dynamic-slice_fusion.3
  181.7 1.2 convolution_convert_fusion.2
  183.7 3.8 %bitcast_add_fusion.2 = f32[128,8,4,128]{0,3,1,2:T(8,128)} fusion(f32[128,8,4,128]{0,3,1,2:T(8,128)} %get-tuple-element.181, bf16[128,8,4,128]{3,2,1,0:T(4,128)(2,1)S(1)} %reshape.59, pred[]{:T(512)S(6)} %compare.7, bf16[1,4,128,128]{3,1,2,0:T(4,128)(2,1)S(1)} %constant_dynamic-slice_fusion.3), kind=kOutput, calls=%fused_computation.1.clone.1 | convolution fusion | flops 135266304 | bytes 5373953 | tf_op jit(solution)/shard_map/while/body/eval_jaxpr/apsd,sbd->apsb/dot_general | solution.py:45
  187.5 0.9 constant_dynamic-slice_fusion.3
  188.4 1.2 convolution_convert_fusion.2
  190.4 3.8 %bitcast_add_fusion.2 = f32[128,8,4,128]{0,3,1,2:T(8,128)} fusion(f32[128,8,4,128]{0,3,1,2:T(8,128)} %get-tuple-element.181, bf16[128,8,4,128]{3,2,1,0:T(4,128)(2,1)S(1)} %reshape.59, pred[]{:T(512)S(6)} %compare.7, bf16[1,4,128,128]{3,1,2,0:T(4,128)(2,1)S(1)} %constant_dynamic-slice_fusion.3), kind=kOutput, calls=%fused_computation.1.clone.1 | convolution fusion | flops 135266304 | bytes 5373953 | tf_op jit(solution)/shard_map/while/body/eval_jaxpr/apsd,sbd->apsb/dot_general | solution.py:45
  194.2 0.9 constant_dynamic-slice_fusion.3
  195.1 1.2 convolution_convert_fusion.2
  197.1 3.8 %bitcast_add_fusion.2 = f32[128,8,4,128]{0,3,1,2:T(8,128)} fusion(f32[128,8,4,128]{0,3,1,2:T(8,128)} %get-tuple-element.181, bf16[128,8,4,128]{3,2,1,0:T(4,128)(2,1)S(1)} %reshape.59, pred[]{:T(512)S(6)} %compare.7, bf16[1,4,128,128]{3,1,2,0:T(4,128)(2,1)S(1)} %constant_dynamic-slice_fusion.3), kind=kOutput, calls=%fused_computation.1.clone.1 | convolution fusion | flops 135266304 | bytes 5373953 | tf_op jit(solution)/shard_map/while/body/eval_jaxpr/apsd,sbd->apsb/dot_general | solution.py:45
  200.9 0.9 constant_dynamic-slice_fusion.3
  201.9 1.2 convolution_convert_fusion.2
  203.8 3.8 %bitcast_add_fusion.2 = f32[128,8,4,128]{0,3,1,2:T(8,128)} fusion(f32[128,8,4,128]{0,3,1,2:T(8,128)} %get-tuple-element.181, bf16[128,8,4,128]{3,2,1,0:T(4,128)(2,1)S(1)} %reshape.59, pred[]{:T(512)S(6)} %compare.7, bf16[1,4,128,128]{3,1,2,0:T(4,128)(2,1)S(1)} %constant_dynamic-slice_fusion.3), kind=kOutput, calls=%fused_computation.1.clone.1 | convolution fusion | flops 135266304 | bytes 5373953 | tf_op jit(solution)/shard_map/while/body/eval_jaxpr/apsd,sbd->apsb/dot_general | solution.py:45
  207.6 0.9 constant_dynamic-slice_fusion.3
  208.6 1.2 convolution_convert_fusion.2
  210.5 3.8 %bitcast_add_fusion.2 = f32[128,8,4,128]{0,3,1,2:T(8,128)} fusion(f32[128,8,4,128]{0,3,1,2:T(8,128)} %get-tuple-element.181, bf16[128,8,4,128]{3,2,1,0:T(4,128)(2,1)S(1)} %reshape.59, pred[]{:T(512)S(6)} %compare.7, bf16[1,4,128,128]{3,1,2,0:T(4,128)(2,1)S(1)} %constant_dynamic-slice_fusion.3), kind=kOutput, calls=%fused_computation.1.clone.1 | convolution fusion | flops 135266304 | bytes 5373953 | tf_op jit(solution)/shard_map/while/body/eval_jaxpr/apsd,sbd->apsb/dot_general | solution.py:45
  215.3 1.2 convolution_convert_fusion.2
  217.3 3.8 %bitcast_add_fusion.2 = f32[128,8,4,128]{0,3,1,2:T(8,128)} fusion(f32[128,8,4,128]{0,3,1,2:T(8,128)} %get-tuple-element.181, bf16[128,8,4,128]{3,2,1,0:T(4,128)(2,1)S(1)} %reshape.59, pred[]{:T(512)S(6)} %compare.7, bf16[1,4,128,128]{3,1,2,0:T(4,128)(2,1)S(1)} %constant_dynamic-slice_fusion.3), kind=kOutput, calls=%fused_computation.1.clone.1 | convolution fusion | flops 135266304 | bytes 5373953 | tf_op jit(solution)/shard_map/while/body/eval_jaxpr/apsd,sbd->apsb/dot_general | solution.py:45
  222.0 1.2 convolution_convert_fusion.2
  224.0 3.8 %bitcast_add_fusion.2 = f32[128,8,4,128]{0,3,1,2:T(8,128)} fusion(f32[128,8,4,128]{0,3,1,2:T(8,128)} %get-tuple-element.181, bf16[128,8,4,128]{3,2,1,0:T(4,128)(2,1)S(1)} %reshape.59, pred[]{:T(512)S(6)} %compare.7, bf16[1,4,128,128]{3,1,2,0:T(4,128)(2,1)S(1)} %constant_dynamic-slice_fusion.3), kind=kOutput, calls=%fused_computation.1.clone.1 | convolution fusion | flops 135266304 | bytes 5373953 | tf_op jit(solution)/shard_map/while/body/eval_jaxpr/apsd,sbd->apsb/dot_general | solution.py:45
  228.7 1.2 convolution_convert_fusion.2
  230.7 3.8 %bitcast_add_fusion.2 = f32[128,8,4,128]{0,3,1,2:T(8,128)} fusion(f32[128,8,4,128]{0,3,1,2:T(8,128)} %get-tuple-element.181, bf16[128,8,4,128]{3,2,1,0:T(4,128)(2,1)S(1)} %reshape.59, pred[]{:T(512)S(6)} %compare.7, bf16[1,4,128,128]{3,1,2,0:T(4,128)(2,1)S(1)} %constant_dynamic-slice_fusion.3), kind=kOutput, calls=%fused_computation.1.clone.1 | convolution fusion | flops 135266304 | bytes 5373953 | tf_op jit(solution)/shard_map/while/body/eval_jaxpr/apsd,sbd->apsb/dot_general | solution.py:45
  235.4 1.2 convolution_convert_fusion.2
  237.4 3.8 %bitcast_add_fusion.2 = f32[128,8,4,128]{0,3,1,2:T(8,128)} fusion(f32[128,8,4,128]{0,3,1,2:T(8,128)} %get-tuple-element.181, bf16[128,8,4,128]{3,2,1,0:T(4,128)(2,1)S(1)} %reshape.59, pred[]{:T(512)S(6)} %compare.7, bf16[1,4,128,128]{3,1,2,0:T(4,128)(2,1)S(1)} %constant_dynamic-slice_fusion.3), kind=kOutput, calls=%fused_computation.1.clone.1 | convolution fusion | flops 135266304 | bytes 5373953 | tf_op jit(solution)/shard_map/while/body/eval_jaxpr/apsd,sbd->apsb/dot_general | solution.py:45
  242.1 1.2 convolution_convert_fusion.2
  244.1 3.8 %bitcast_add_fusion.2 = f32[128,8,4,128]{0,3,1,2:T(8,128)} fusion(f32[128,8,4,128]{0,3,1,2:T(8,128)} %get-tuple-element.181, bf16[128,8,4,128]{3,2,1,0:T(4,128)(2,1)S(1)} %reshape.59, pred[]{:T(512)S(6)} %compare.7, bf16[1,4,128,128]{3,1,2,0:T(4,128)(2,1)S(1)} %constant_dynamic-slice_fusion.3), kind=kOutput, calls=%fused_computation.1.clone.1 | convolution fusion | flops 135266304 | bytes 5373953 | tf_op jit(solution)/shard_map/while/body/eval_jaxpr/apsd,sbd->apsb/dot_general | solution.py:45
  248.9 1.2 convolution_convert_fusion.2
  250.8 3.8 %bitcast_add_fusion.2 = f32[128,8,4,128]{0,3,1,2:T(8,128)} fusion(f32[128,8,4,128]{0,3,1,2:T(8,128)} %get-tuple-element.181, bf16[128,8,4,128]{3,2,1,0:T(4,128)(2,1)S(1)} %reshape.59, pred[]{:T(512)S(6)} %compare.7, bf16[1,4,128,128]{3,1,2,0:T(4,128)(2,1)S(1)} %constant_dynamic-slice_fusion.3), kind=kOutput, calls=%fused_computation.1.clone.1 | convolution fusion | flops 135266304 | bytes 5373953 | tf_op jit(solution)/shard_map/while/body/eval_jaxpr/apsd,sbd->apsb/dot_general | solution.py:45
  255.6 1.2 convolution_convert_fusion.2
  257.5 3.8 %bitcast_add_fusion.2 = f32[128,8,4,128]{0,3,1,2:T(8,128)} fusion(f32[128,8,4,128]{0,3,1,2:T(8,128)} %get-tuple-element.181, bf16[128,8,4,128]{3,2,1,0:T(4,128)(2,1)S(1)} %reshape.59, pred[]{:T(512)S(6)} %compare.7, bf16[1,4,128,128]{3,1,2,0:T(4,128)(2,1)S(1)} %constant_dynamic-slice_fusion.3), kind=kOutput, calls=%fused_computation.1.clone.1 | convolution fusion | flops 135266304 | bytes 5373953 | tf_op jit(solution)/shard_map/while/body/eval_jaxpr/apsd,sbd->apsb/dot_general | solution.py:45
  261.3 3.1 copy.16
  264.5 8.6 %all-to-all-start = ((f32[16,8,8,4,128]{4,2,3,1,0:T(8,128)}), f32[16,8,8,4,128]{4,2,3,1,0:T(8,128)S(1)}, u32[]{:S(2)}, u32[]{:S(2)}) async-start(f32[16,8,8,4,128]{4,2,3,1,0:T(8,128)} %bitcast.33), calls=%async_computation | async-start | bytes 4194304 | tf_op jit(solution)/shard_map/all_to_all | solution.py:14
  274.3 49.9 %all-to-all-done = f32[16,8,8,4,128]{4,2,3,1,0:T(8,128)S(1)} async-done(((f32[16,8,8,4,128]{4,2,3,1,0:T(8,128)}), f32[16,8,8,4,128]{4,2,3,1,0:T(8,128)S(1)}, u32[]{:S(2)}, u32[]{:S(2)}) %all-to-all-start) | async-done | bytes 2097184 | tf_op jit(solution)/shard_map/all_to_all | solution.py:14
  (42 shorter events, 22.7 us)
Async XLA Ops:
  7.2 2.6 copy-start
  7.2 131.7 %all-gather.2.cloned.1.call-start = ((), (), s32[]{:S(2)}) async-start(), calls=%async_computation.1 | async-start | bytes 17301504 | tf_op jit(solution)/shard_map/all_gather | solution.py:28
  264.5 8.6 %copy-start.2 = (f32[4096]{0:T(1024)S(1)}, f32[4096]{0:T(1024)}, u32[]{:S(2)}) copy-start(f32[4096]{0:T(1024)} %param.9) | copy-start | bytes 49156
  264.5 59.7 %all-to-all-start = ((f32[16,8,8,4,128]{4,2,3,1,0:T(8,128)}), f32[16,8,8,4,128]{4,2,3,1,0:T(8,128)S(1)}, u32[]{:S(2)}, u32[]{:S(2)}) async-start(f32[16,8,8,4,128]{4,2,3,1,0:T(8,128)} %bitcast.33), calls=%async_computation | async-start | bytes 4194304 | tf_op jit(solution)/shard_map/all_to_all | solution.py:14
  273.0 52.0 %copy-start.1 = (f32[8]{0:T(128)S(1)}, f32[8]{0:T(128)}, u32[]{:S(2)}) copy-start(f32[8]{0:T(128)} %param.10) | copy-start | bytes 100
Sparse Core Ops, SparseCore 0:
  11.2 127.5 all-gather.1
where the time goes:
time: 335 us; the launch traced here: 333 us
  waiting for transfers between devices  179 us (53%)
  matrix products  94.9 us (28%)
  local copies, waits for them, and re-layouts  34.7 us (10%)
  between operations  14.1 us (4%)
  starting transfers between devices  8.6 us (3%)
    all_gather x1, waiting for transfers between devices, local(): piece = lax.all_gather(integrals, 'blk', axis=1, tiled=True)  129 us
    dot_general x16, matrix products, add_aux(): jnp.einsum('apsd,sbd->apsb', half_split, col_blocks[aux], preferred_eleme...  59.2 us
    all_to_all x1, waiting for transfers between devices, sum_at_owner(): blocks = lax.all_to_all(in_blocks(x, dim, devices), axis, 0, 0, tiled=True)  49.9 us
    dot_general x16, matrix products, add_aux(): jnp.dot(integrals[aux], flattened_rows, preferred_element_type=jnp.float32)  18.9 us
    dot_general x1, matrix products, local(): jnp.einsum('sj,qjbd->qsbd', onehot, pieces, preferred_element_type=jnp.fl...  16.6 us
    dynamic_slice x16, local copies, waits for them, and re-layouts, add_aux(): col_blocks[aux]  15.2 us
    reshape x16, local copies, waits for them, and re-layouts, add_aux(): half_split.reshape(rows_per_device * lax.axis_size('grp'), pair_count, sl...  12.2 us
    all_to_all x1, starting transfers between devices, sum_at_owner(): blocks = lax.all_to_all(in_blocks(x, dim, devices), axis, 0, 0, tiled=True)  8.57 us
  transfers between devices with their start and end apart: 2, of which 2 were waited for; matrix products, arithmetic and copies ran while one was open for 1% of the time, Pallas kernels for 0%

commit v1 on v0

--- a/solution.py
+++ b/solution.py
@@ -2,6 +2,7 @@
 import jax.numpy as jnp
 from jax import lax
 from jax.sharding import PartitionSpec as P
+from jax.lax import all_to_all, psum
 
 
 def in_blocks(x, dim, devices):
@@ -25,7 +26,15 @@
     slot_count = amplitudes.shape[2]
     own_offsets = lax.dynamic_slice_in_dim(offsets, tile_index, 1, 0)[0]
     cols = (tile_index - own_offsets) % tiles
-    piece = lax.all_gather(integrals, "blk", axis=1, tiled=True)
+    piece = jnp.concatenate(
+        all_to_all(
+            jnp.stack(psum(1, axis_name="blk") * [integrals], axis=0),
+            concat_axis=0,
+            axis_name="blk",
+            split_axis=0,
+        ),
+        axis=1,
+    )
     count = piece.shape[1] // slab_width
     tile_ids = jnp.arange(count, dtype=jnp.int32)
     onehot = (cols[:, None] == tile_ids[None, :]).astype(jnp.bfloat16)

time: 335 us -> 577 us (1.72)
  the two profiles are of different devices: /device:TPU:2 before, /device:TPU:7 now
where the time goes in v1:
time: 577 us; the launch traced here: 575 us
  waiting for transfers between devices  414 us (72%)
  matrix products  95.1 us (16%)
  local copies, waits for them, and re-layouts  40.9 us (7%)
  starting transfers between devices  23.5 us (4%)
    all_to_all x1, waiting for transfers between devices, local(): all_to_all(jnp.stack(psum(1, axis_name='blk') * [integrals], axis=0), con...  363 us
    dot_general x16, matrix products, add_aux(): jnp.einsum('apsd,sbd->apsb', half_split, col_blocks[aux], preferred_eleme...  59.4 us
    all_to_all x1, waiting for transfers between devices, sum_at_owner(): blocks = lax.all_to_all(in_blocks(x, dim, devices), axis, 0, 0, tiled=True)  50.5 us
    dot_general x16, matrix products, add_aux(): jnp.dot(integrals[aux], flattened_rows, preferred_element_type=jnp.float32)  18.8 us
    dot_general x1, matrix products, local(): jnp.einsum('sj,qjbd->qsbd', onehot, pieces, preferred_element_type=jnp.fl...  16.6 us
    dynamic_slice x16, local copies, waits for them, and re-layouts, add_aux(): col_blocks[aux]  15.3 us
    all_to_all x1, starting transfers between devices, sum_at_owner(): blocks = lax.all_to_all(in_blocks(x, dim, devices), axis, 0, 0, tiled=True)  12.3 us
    reshape x16, local copies, waits for them, and re-layouts, add_aux(): half_split.reshape(rows_per_device * lax.axis_size('grp'), pair_count, sl...  12.2 us
  transfers between devices with their start and end apart: 2, of which 2 were waited for; matrix products, arithmetic and copies ran while one was open for 0% of the time, Pallas kernels for 0%

profile of v1, /device:TPU:7, one launch (start us, length us, event | category | flops | bytes accessed | tf_op | source)
XLA Modules:
  0.0 574.6 jit_solution(11668012332613712778)
XLA Ops:
  0.6 7.0 %stack.2 = bf16[32,16,128,128]{3,2,1,0:T(8,128)(2,1)} broadcast(bf16[16,128,128]{2,1,0:T(8,128)(2,1)} %param.8), dimensions={1,2,3} | broadcast | bytes 17301504 | tf_op jit(solution)/shard_map/stack | solution.py:31
  7.7 11.1 %all-to-all-start = ((bf16[32,16,128,128]{3,2,1,0:T(8,128)(2,1)}), bf16[32,16,128,128]{3,2,1,0:T(8,128)(2,1)}, u32[]{:S(2)}, u32[]{:S(2)}) async-start(bf16[32,16,128,128]{3,2,1,0:T(8,128)(2,1)} %stack.2), calls=%async_computation | async-start | bytes 33554432 | tf_op jit(solution)/shard_map/all_to_all | solution.py:30
  19.9 363.1 %all-to-all-done = bf16[32,16,128,128]{3,2,1,0:T(8,128)(2,1)} async-done(((bf16[32,16,128,128]{3,2,1,0:T(8,128)(2,1)}), bf16[32,16,128,128]{3,2,1,0:T(8,128)(2,1)}, u32[]{:S(2)}, u32[]{:S(2)}) %all-to-all-start) | async-done | bytes 16777248 | tf_op jit(solution)/shard_map/all_to_all | solution.py:30
  383.0 16.6 %convert_bitcast_fusion = bf16[16,4,128,128]{3,1,2,0:T(4,128)(2,1)} fusion(bf16[32,16,128,128]{3,2,1,0:T(8,128)(2,1)} %all-to-all-done, s32[4]{0:T(128)S(1)} %and_select_fusion), kind=kOutput, calls=%fused_computation.11 | convolution fusion | flops 68157568 | bytes 18874384 | tf_op jit(solution)/shard_map/sj,qjbd->qsbd/dot_general | solution.py:42
  399.6 106.2 %while.14 = (s32[]{:T(128)}, f32[128,8,4,128]{0,3,1,2:T(8,128)}, bf16[16,4,128,128]{3,1,2,0:T(4,128)(2,1)}, bf16[16,128,128]{2,1,0:T(8,128)(2,1)}, bf16[128,4096]{1,0:T(8,128)(2,1)S(1)}, /*index=5*/s32[]{:T(128)}, s32[]{:T(128)}) while((s32[]{:T(128)}, f32[128,8,4,128]{0,3,1,2:T(8,128)}, bf16[16,4,128,128]{3,1,2,0:T(4,128)(2,1)}, ...), condition=%wide.region_1.2_spmd.clone, body=%wide.region_0.1_spmd.clone.sunk | while | flops 270008320 | bytes 9863771 | solution.py:61
  399.6 1.2 convolution_convert_fusion.2
  401.6 1.0 constant_dynamic-slice_fusion.3
  402.5 2.2 bitcast_add_fusion.2
  404.8 1.2 convolution_convert_fusion.2
  406.7 1.0 constant_dynamic-slice_fusion.3
  407.7 3.8 bitcast_add_fusion.2
  411.5 1.2 convolution_convert_fusion.2
  414.4 3.8 bitcast_add_fusion.2
  418.2 1.2 convolution_convert_fusion.2
  420.2 1.0 constant_dynamic-slice_fusion.3
  421.2 3.8 bitcast_add_fusion.2
  425.0 1.2 convolution_convert_fusion.2
  427.9 3.8 bitcast_add_fusion.2
  431.7 1.2 convolution_convert_fusion.2
  433.7 1.0 constant_dynamic-slice_fusion.3
  434.6 3.8 bitcast_add_fusion.2
  438.5 1.2 convolution_convert_fusion.2
  440.4 1.0 constant_dynamic-slice_fusion.3
  441.4 3.8 bitcast_add_fusion.2
  445.2 1.2 convolution_convert_fusion.2
  448.1 3.8 bitcast_add_fusion.2
  451.9 1.2 convolution_convert_fusion.2
  453.9 1.0 constant_dynamic-slice_fusion.3
  454.9 3.8 bitcast_add_fusion.2
  458.7 1.2 convolution_convert_fusion.2
  461.6 3.8 bitcast_add_fusion.2
  465.4 1.2 convolution_convert_fusion.2
  468.3 3.8 bitcast_add_fusion.2
  472.1 1.2 convolution_convert_fusion.2
  475.1 3.8 bitcast_add_fusion.2
  478.9 1.2 convolution_convert_fusion.2
  481.8 3.8 bitcast_add_fusion.2
  485.6 1.2 convolution_convert_fusion.2
  487.6 1.0 constant_dynamic-slice_fusion.3
  488.5 3.8 bitcast_add_fusion.2
  492.4 1.2 convolution_convert_fusion.2
  495.3 3.8 bitcast_add_fusion.2
  499.1 1.2 convolution_convert_fusion.2
  501.0 1.0 constant_dynamic-slice_fusion.3
  502.0 3.8 bitcast_add_fusion.2
  505.8 3.1 copy.15
  508.9 12.3 %all-to-all-start.1 = ((f32[16,8,8,4,128]{4,2,3,1,0:T(8,128)}), f32[16,8,8,4,128]{4,2,3,1,0:T(8,128)S(1)}, u32[]{:S(2)}, u32[]{:S(2)}) async-start(f32[16,8,8,4,128]{4,2,3,1,0:T(8,128)} %bitcast.36), calls=%async_computation.1 | async-start | bytes 4194304 | tf_op jit(solution)/shard_map/all_to_all | solution.py:15
  522.5 50.5 %all-to-all-done.1 = f32[16,8,8,4,128]{4,2,3,1,0:T(8,128)S(1)} async-done(((f32[16,8,8,4,128]{4,2,3,1,0:T(8,128)}), f32[16,8,8,4,128]{4,2,3,1,0:T(8,128)S(1)}, u32[]{:S(2)}, u32[]{:S(2)}) %all-to-all-start.1) | async-done | bytes 2097184 | tf_op jit(solution)/shard_map/all_to_all | solution.py:15
  (44 shorter events, 23.8 us)
Async XLA Ops:
  7.7 11.2 %copy-start = (bf16[128,8,4,128]{3,2,1,0:T(4,128)(2,1)S(1)}, bf16[128,8,4,128]{3,2,1,0:T(4,128)(2,1)}, u32[]{:S(2)}) copy-start(bf16[128,8,4,128]{3,2,1,0:T(4,128)(2,1)} %param.7) | copy-start | bytes 3145732
  7.7 375.3 %all-to-all-start = ((bf16[32,16,128,128]{3,2,1,0:T(8,128)(2,1)}), bf16[32,16,128,128]{3,2,1,0:T(8,128)(2,1)}, u32[]{:S(2)}, u32[]{:S(2)}) async-start(bf16[32,16,128,128]{3,2,1,0:T(8,128)(2,1)} %stack.2), calls=%async_computation | async-start | bytes 33554432 | tf_op jit(solution)/shard_map/all_to_all | solution.py:30
  18.8 0.9 copy-start.1
  508.9 12.3 %copy-start.3 = (f32[4096]{0:T(1024)S(1)}, f32[4096]{0:T(1024)}, u32[]{:S(2)}) copy-start(f32[4096]{0:T(1024)} %param.9) | copy-start | bytes 49156
  508.9 64.0 %all-to-all-start.1 = ((f32[16,8,8,4,128]{4,2,3,1,0:T(8,128)}), f32[16,8,8,4,128]{4,2,3,1,0:T(8,128)S(1)}, u32[]{:S(2)}, u32[]{:S(2)}) async-start(f32[16,8,8,4,128]{4,2,3,1,0:T(8,128)} %bitcast.36), calls=%async_computation.1 | async-start | bytes 4194304 | tf_op jit(solution)/shard_map/all_to_all | solution.py:15
  521.3 52.6 %copy-start.2 = (f32[8]{0:T(128)S(1)}, f32[8]{0:T(128)}, u32[]{:S(2)}) copy-start(f32[8]{0:T(128)} %param.10) | copy-start | bytes 100
